TPU v7x, 512 devices: a whole 4x4x16 slice. The times are simulated.
512 devices in a mesh: row: 32 (over z, core), col: 16 (over x, y).
Axes of the slice: x: 4, y: 4, z: 16, core: 2. Of those that a mesh axis runs over, the one named last changes fastest.
Arguments:
- front_entries: float32 [16384, 16384], P('row', 'col'), may hold values from 0 to 3, as said below
- tile_group: int32 [32], replicated, may hold values from 0 to 3
- child_factor: bfloat16 [16384, 256], P('row', 'col'), may hold values from -0.375 to 0.375
- row_map: int32 [128], replicated, may hold values from 0 to 127, as said below
Outputs:
- factor_panels: bfloat16 [16384, 512], P('row', 'col')
- schur_block: float32 [16384, 16384], P('row', 'col')
Inputs may be any that keep to these rules, and one draw needn't show every extreme that they name: `front_entries`: Symmetric; assembled is positive definite. `row_map`: A permutation of the parent tiles. The tile in row block r (blocks of 512 rows) goes to a parent tile in row block r or in the row block whose index differs from r in the highest bit.
All inputs are finite; a program needn't handle non-finite values.
Results may differ from a plain program's by a relative error of at most 0.0026.
Values may be sent and summed in bfloat16 or wider, within the bound.
A program may use at most 64 MiB of HBM per device.

v0:
```python
import jax
import jax.numpy as jnp
from jax import lax
from jax.sharding import PartitionSpec as P

PW = 256
NP = 2
TS = 128
MT = 512


def swapped(value, axis, stride):
    mask = 2**stride
    pairs = [(source, source ^ mask) for source in range(lax.axis_size(axis))]
    return lax.ppermute(value, axis, pairs)


def broadcast(value, axis, source):
    kept = jnp.where(lax.axis_index(axis) == source, value, 0).astype(value.dtype)
    return lax.psum(kept, axis)


def panel_columns(matrix, offset, width_cols, fan_ratio, block_rows):
    return jnp.concatenate(
        [
            matrix[:, q * block_rows + offset : q * block_rows + offset + width_cols]
            for q in range(fan_ratio)
        ],
        axis=1,
    )


def outer_rows(left, right):
    return jnp.einsum("ik,jk->ij", left, right, preferred_element_type=jnp.float32)


def subtract_block(matrix, lead_rows, owner, low, col_from, col_to, base_col):
    region = matrix[low:, base_col + col_from : base_col + col_to]
    return matrix.at[low:, base_col + col_from : base_col + col_to].set(
        region - outer_rows(lead_rows, owner[col_from:col_to])
    )


def right_solve(lower_factor, strip):
    return lax.linalg.triangular_solve(
        lower_factor, strip, left_side=False, lower=True, transpose_a=True
    )


def local(front_entries, tile_group, child_factor, row_map):
    row_count = lax.axis_size("row")
    col_count = lax.axis_size("col")
    fan_ratio = row_count // col_count
    local_rows = front_entries.shape[0]
    local_cols = front_entries.shape[1]
    my_row = lax.axis_index("row")
    my_col = lax.axis_index("col")
    row_tiles = local_rows // MT
    col_tiles = local_cols // MT
    group_rows = lax.dynamic_slice_in_dim(tile_group, my_row * row_tiles, row_tiles)
    group_cols = lax.dynamic_slice_in_dim(tile_group, my_col * col_tiles, col_tiles)
    same_group = (group_rows[:, None] == group_cols[None, :]).astype(jnp.float32)
    masked = (
        front_entries.reshape(row_tiles, MT, col_tiles, MT) * same_group[:, None, :, None]
    ).reshape(local_rows, local_cols)
    child_full = lax.all_gather(child_factor, "col", axis=1, tiled=True)
    child_width = child_full.shape[1]
    partner_full = swapped(child_full, "row", row_count.bit_length() - 2)
    tile_count = local_rows // TS
    partner_row = jnp.bitwise_xor(my_row, row_count // 2)
    own_map = lax.dynamic_slice_in_dim(row_map, my_row * tile_count, tile_count)
    partner_map = lax.dynamic_slice_in_dim(row_map, partner_row * tile_count, tile_count)
    slot_ids = my_row * tile_count + jnp.arange(tile_count, dtype=jnp.int32)

    def place_tiles(tile_map, source):
        chooser = (tile_map[None, :] == slot_ids[:, None]).astype(jnp.bfloat16)
        placed = jnp.dot(
            chooser,
            source.reshape(tile_count, TS * child_width),
            preferred_element_type=jnp.float32,
        )
        return placed.astype(jnp.bfloat16).reshape(local_rows, child_width)

    own_parent = place_tiles(own_map, child_full)
    partner_parent = place_tiles(partner_map, partner_full)
    lower_half = my_row < row_count // 2
    child_wide = jnp.where(
        lower_half,
        jnp.concatenate([own_parent, partner_parent], axis=1),
        jnp.concatenate([partner_parent, own_parent], axis=1),
    )
    child_owners = [broadcast(child_wide, "row", fan_ratio * my_col + q) for q in range(fan_ratio)]
    matrix = jnp.concatenate(
        [
            masked[:, q * local_rows : (q + 1) * local_rows]
            + outer_rows(child_wide, child_owners[q])
            for q in range(fan_ratio)
        ],
        axis=1,
    )
    row_share = PW // row_count
    col_share = PW // col_count
    local_ids = jnp.arange(local_rows)
    coming = None
    outputs = []
    for k in range(NP):
        offset = k * row_share
        panel_strip = panel_columns(matrix, offset, row_share, fan_ratio, local_rows)
        corner = panel_strip[offset : offset + row_share]
        gathered = lax.all_gather(corner, ("row", "col"), axis=0, tiled=True)
        diagonal = (
            gathered.reshape(row_count, col_count, row_share, col_share)
            .transpose(0, 2, 1, 3)
            .reshape(PW, PW)
        )
        lower_factor = jnp.linalg.cholesky(diagonal)
        whole_strip = lax.all_gather(panel_strip, "col", axis=1, tiled=True)
        rounded = right_solve(lower_factor, whole_strip).astype(jnp.bfloat16)
        own_lower = lax.dynamic_slice_in_dim(lower_factor, my_row * row_share, row_share).astype(
            jnp.bfloat16
        )
        rounded = jnp.where((local_ids < offset)[:, None], jnp.zeros_like(rounded), rounded)
        rounded = rounded.at[offset : offset + row_share].set(own_lower)
        outputs.append(lax.dynamic_slice_in_dim(rounded, my_col * col_share, col_share, 1))
        owners = [broadcast(rounded, "row", fan_ratio * my_col + q) for q in range(fan_ratio)]
        low = offset + row_share
        lead_rows = rounded[low:]
        for q in range(fan_ratio):
            matrix = subtract_block(
                matrix, lead_rows, owners[q], low, low, local_rows, q * local_rows
            )
    pivot_done = NP * row_share
    row_keep = local_ids >= pivot_done
    col_keep = jnp.arange(local_cols) % local_rows >= pivot_done
    schur_block = jnp.where(row_keep[:, None] & col_keep[None, :], matrix, jnp.zeros_like(matrix))
    factor_panels = jnp.concatenate(outputs, axis=1)
    return (factor_panels, schur_block)


def solution(mesh):
    placed = (P("row", "col"), P(), P("row", "col"), P())
    return jax.shard_map(
        local,
        mesh=mesh,
        in_specs=placed,
        out_specs=(P("row", "col"), P("row", "col")),
        check_vma=False,
    )
```

profile of v0, /device:TPU:1, one launch (start us, length us, event | category | flops | bytes accessed | tf_op | source)
XLA Modules:
  0.0 1302.7 jit_solution(17513636110733798873)
XLA Ops:
  7.2 19.7 %all_gather.15 = bf16[512,256]{0,1:T(8,128)(2,1)S(1)} all-gather(bf16[512,16]{0,1:T(8,128)(2,1)} %param.21), channel_id=1, replica_groups=mesh['row'=32,'col'=16] {'col'}, dimensions={1}, use_global_device_ids=true | all-gather | bytes 278528 | tf_op jit(solution)/shard_map/all_gather | solution.py:66
  26.9 15.4 %collective-permute-start = (bf16[512,256]{0,1:T(8,128)(2,1)S(1)}, bf16[512,256]{0,1:T(8,128)(2,1)S(1)}, u32[]{:S(2)}, u32[]{:S(2)}) collective-permute-start(bf16[512,256]{0,1:T(8,128)(2,1)S(1)} %all_gather.15), channel_id=1, source_target_pairs={{0,256},{16,272},{32,288},{48,304},{64,320},{80,336},{96,352},{112... | collective-permute-start | bytes 786440 | tf_op jit(solution)/shard_map/ppermute | solution.py:15
  51.2 226.5 %all-reduce.12.cloned.1.call-done = (bf16[512,512]{1,0:T(8,128)(2,1)}, bf16[512,512]{1,0:T(8,128)(2,1)}) async-done(((bf16[512,512]{1,0:T(8,128)(2,1)}, bf16[512,512]{1,0:T(8,128)(2,1)}), (bf16[512,512]{1,0:T(8,128)(2,1)}, bf16[512,512]{1,0:T(8,128)(2,1)})) %all-reduce.12.cloned.1.call-update) | async-done | bytes 1048592 | tf_op jit(solution)/shard_map/psum | solution.py:20
  281.4 198.2 %all_gather.16 = f32[4096,16]{1,0:T(8,128)S(1)} all-gather(f32[8,16]{1,0:T(8,128)S(1)} %copy.33), channel_id=1, replica_groups=mesh['row'=32,'col'=16] {'row','col'}, dimensions={0}, use_global_device_ids=true | all-gather | bytes 262656 | tf_op jit(solution)/shard_map/all_gather | solution.py:110
  481.1 11.7 cholesky.130
  492.8 9.8 custom-call.13
  503.1 11.9 cholesky.147
  517.6 3.8 while.10
  521.5 19.7 %custom-call.14 = f32[2,128,128]{1,2,0:T(8,128)S(1)} custom-call(f32[2,128,128]{2,1,0:T(8,128)S(1)} %get-tuple-element.90), custom_call_target="InvertDiagBlocksLowerTriangular" | custom-call | tf_op jit(solution)/shard_map/triangular_solve/custom-call.0 | solution.py:45
  541.2 16.2 %all_gather.17 = f32[512,256]{0,1:T(8,128)S(1)} all-gather(f32[512,16]{0,1:T(8,128)S(1)} %pad_maximum_fusion.1), channel_id=1, replica_groups=mesh['row'=32,'col'=16] {'col'}, dimensions={1}, use_global_device_ids=true | all-gather | bytes 557056 | tf_op jit(solution)/shard_map/all_gather | solution.py:117
  561.5 209.2 %all-reduce.10.cloned.1.call-done = (bf16[512,256]{0,1:T(8,128)(2,1)}, bf16[512,256]{0,1:T(8,128)(2,1)}) async-done(((bf16[512,256]{0,1:T(8,128)(2,1)}, bf16[512,256]{0,1:T(8,128)(2,1)}), (bf16[512,256]{0,1:T(8,128)(2,1)}, bf16[512,256]{0,1:T(8,128)(2,1)})) %all-reduce.10.cloned.1.call-update) | async-done | bytes 524304 | tf_op jit(solution)/shard_map/psum | solution.py:20
  773.2 5.4 scatter.21
  780.2 3.4 scatter.24
  783.8 197.6 %all_gather.18 = f32[4096,16]{1,0:T(8,128)S(1)} all-gather(f32[8,16]{1,0:T(8,128)S(1)} %copy.38), channel_id=1, replica_groups=mesh['row'=32,'col'=16] {'row','col'}, dimensions={0}, use_global_device_ids=true | all-gather | bytes 262656 | tf_op jit(solution)/shard_map/all_gather | solution.py:110
  986.0 11.7 cholesky.164
  997.8 9.8 custom-call.15
  1008.1 11.7 cholesky.181
  1022.4 4.0 while.11
  1026.5 19.9 %custom-call.16 = f32[2,128,128]{1,2,0:T(8,128)S(1)} custom-call(f32[2,128,128]{2,1,0:T(8,128)S(1)} %get-tuple-element.91), custom_call_target="InvertDiagBlocksLowerTriangular" | custom-call | tf_op jit(solution)/shard_map/triangular_solve/custom-call.0 | solution.py:45
  1046.4 16.3 %all_gather.19 = f32[512,256]{0,1:T(8,128)S(1)} all-gather(f32[512,16]{0,1:T(8,128)S(1)} %pad_maximum_fusion.2), channel_id=1, replica_groups=mesh['row'=32,'col'=16] {'col'}, dimensions={1}, use_global_device_ids=true | all-gather | bytes 557056 | tf_op jit(solution)/shard_map/all_gather | solution.py:117
  1066.2 210.0 %all-reduce.8.cloned.1.call-done = (bf16[512,256]{0,1:T(8,128)(2,1)}, bf16[512,256]{0,1:T(8,128)(2,1)}) async-done(((bf16[512,256]{0,1:T(8,128)(2,1)}, bf16[512,256]{0,1:T(8,128)(2,1)}), (bf16[512,256]{0,1:T(8,128)(2,1)}, bf16[512,256]{0,1:T(8,128)(2,1)})) %all-reduce.8.cloned.1.call-update) | async-done | bytes 524304 | tf_op jit(solution)/shard_map/psum | solution.py:20
  1278.8 5.4 scatter.26
  1285.8 5.6 scatter.29
  1293.0 2.9 copy.45
  (118 shorter events, 47.5 us)
Async XLA Ops:
  7.2 36.9 %copy-start.5 = (s32[32]{0:T(128)S(1)}, s32[32]{0:T(128)}, u32[]{:S(2)}) copy-start(s32[32]{0:T(128)} %param.20) | copy-start | bytes 388
  7.2 270.5 %all-reduce.12.cloned.1.call-start = ((), (), s32[]{:S(2)}) async-start(), calls=%async_computation.2 | async-start | bytes 2097152 | tf_op jit(solution)/shard_map/psum | solution.py:20
  26.9 20.5 %collective-permute-start = (bf16[512,256]{0,1:T(8,128)(2,1)S(1)}, bf16[512,256]{0,1:T(8,128)(2,1)S(1)}, u32[]{:S(2)}, u32[]{:S(2)}) collective-permute-start(bf16[512,256]{0,1:T(8,128)(2,1)S(1)} %all_gather.15), channel_id=1, source_target_pairs={{0,256},{16,272},{32,288},{48,304},{64,320},{80,336},{96,352},{112... | collective-permute-start | bytes 786440 | tf_op jit(solution)/shard_map/ppermute | solution.py:15
  48.3 2.9 copy-start.2
  49.6 721.1 %all-reduce.10.cloned.1.call-start = ((), (), s32[]{:S(2)}) async-start(), calls=%async_computation.1 | async-start | bytes 1048576 | tf_op jit(solution)/shard_map/psum | solution.py:20
  51.2 228.6 %copy-start = (f32[512,1024]{0,1:T(8,128)S(1)}, f32[512,1024]{0,1:T(8,128)}, u32[]{:S(2)}) copy-start(f32[512,1024]{0,1:T(8,128)} %broadcast_multiply_fusion) | copy-start | bytes 6291460
  277.7 2.1 copy-start.3
  277.7 2.1 copy-start.6
  280.3 1.0 copy-start.1
  560.0 716.2 %all-reduce.8.cloned.1.call-start = ((), (), s32[]{:S(2)}) async-start(), calls=%async_computation | async-start | bytes 1048576 | tf_op jit(solution)/shard_map/psum | solution.py:20
  1276.2 8.0 copy-start.4
Sparse Core Ops, SparseCore 0:
  49.7 227.9 all-reduce.11
  560.1 210.4 all-reduce.9
  1065.7 210.4 all-reduce.7
where the time goes:
time: 1310 us; the launch traced here: 1300 us
  waiting for transfers between devices  646 us (49%)
  blocking collectives  448 us (34%)
  other arithmetic  119 us (9%)
  local copies, waits for them, and re-layouts  42.4 us (3%)
  between operations  17.1 us (1%)
  starting transfers between devices  15.5 us (1%)
  matrix products  15 us (1%)
    psum x3, waiting for transfers between devices, broadcast(): return lax.psum(kept, axis)  646 us
    all_gather x2, blocking collectives, local(): gathered = lax.all_gather(corner, ('row', 'col'), axis=0, tiled=True)  396 us
    another operation x14, other arithmetic, local(): lower_factor = jnp.linalg.cholesky(diagonal)  69.3 us
    another operation x5, other arithmetic, right_solve(): lax.linalg.triangular_solve(lower_factor, strip, left_side=False, lower=T...  39.7 us
    all_gather x2, blocking collectives, local(): whole_strip = lax.all_gather(panel_strip, 'col', axis=1, tiled=True)  32.5 us
  transfers between devices with their start and end apart: 4, of which 3 were waited for; matrix products, arithmetic and copies ran while one was open for 1% of the time, Pallas kernels for 0%

commit v1 on v0

--- a/solution.py
+++ b/solution.py
@@ -7,6 +7,22 @@
 NP = 2
 TS = 128
 MT = 512
+
+
+def lots_all_treat(block_here):
+    n_blocks = lax.axis_size("col")
+    pool = tuple(((u, (u + 1) % n_blocks) for u in range(n_blocks)))
+    leaves = tuple(((u, (u - 1) % n_blocks) for u in range(n_blocks)))
+    y_new, r2 = ([block_here], [block_here])
+    for _ in range(n_blocks // 2):
+        y_new.append(lax.ppermute(y_new[-1], "col", pool))
+    for _ in range((n_blocks - 1) // 2):
+        r2.append(lax.ppermute(r2[-1], "col", leaves))
+    return jnp.roll(
+        jnp.concatenate([*y_new[::-1], *r2[1:]], axis=1),
+        (lax.axis_index("col") - n_blocks // 2) * block_here.shape[1],
+        axis=1,
+    )
 
 
 def swapped(value, axis, stride):
@@ -114,7 +130,7 @@
             .reshape(PW, PW)
         )
         lower_factor = jnp.linalg.cholesky(diagonal)
-        whole_strip = lax.all_gather(panel_strip, "col", axis=1, tiled=True)
+        whole_strip = lots_all_treat(panel_strip)
         rounded = right_solve(lower_factor, whole_strip).astype(jnp.bfloat16)
         own_lower = lax.dynamic_slice_in_dim(lower_factor, my_row * row_share, row_share).astype(
             jnp.bfloat16

time: 1310 us -> 1400 us (1.069)
  starting transfers between devices: 15.5 us -> 142 us
  blocking collectives: 448 us -> 409 us
    ppermute x0 -> x30, starting transfers between devices: none -> 127 us  [the longest x14 91.1 us: lots_all_treat(): r2.append(lax.ppermute(r2[-1], 'col', leaves))]
    all_gather x2 -> x0, blocking collectives: 32.5 us -> none  [local(): whole_strip = lax.all_gather(panel_strip, 'col', axis=1, tiled=True)]
  transfers between devices with their start and end apart: 4 -> 34, of which waited for: 3 -> 5; matrix products, arithmetic and copies ran while one was open for 1% -> 10% of each run, Pallas kernels for 0% -> 0%
where the time goes in v1:
time: 1400 us
  waiting for transfers between devices  651 us (46%)
  blocking collectives  409 us (29%)
  starting transfers between devices  142 us (10%)
  other arithmetic  119 us (8%)
  local copies, waits for them, and re-layouts  43.3 us (3%)
  between operations  17.8 us (1%)
  matrix products  15 us (1%)
    psum x3, waiting for transfers between devices, broadcast(): return lax.psum(kept, axis)  650 us
    all_gather x2, blocking collectives, local(): gathered = lax.all_gather(corner, ('row', 'col'), axis=0, tiled=True)  389 us
    ppermute x14, starting transfers between devices, lots_all_treat(): r2.append(lax.ppermute(r2[-1], 'col', leaves))  91.1 us
    another operation x14, other arithmetic, local(): lower_factor = jnp.linalg.cholesky(diagonal)  69.2 us
    another operation x5, other arithmetic, right_solve(): lax.linalg.triangular_solve(lower_factor, strip, left_side=False, lower=T...  39.4 us
    ppermute x16, starting transfers between devices, lots_all_treat(): y_new.append(lax.ppermute(y_new[-1], 'col', pool))  35.6 us
  transfers between devices with their start and end apart: 34, of which 5 were waited for; matrix products, arithmetic and copies ran while one was open for 10% of the time, Pallas kernels for 0%

profile of v1, /device:TPU:1, one launch (start us, length us, event | category | flops | bytes accessed | tf_op | source)
XLA Modules:
  0.0 1397.0 jit_solution(11472560034165706275)
XLA Ops:
  7.2 19.7 %all_gather.9 = bf16[512,256]{0,1:T(8,128)(2,1)S(1)} all-gather(bf16[512,16]{0,1:T(8,128)(2,1)} %param.23), channel_id=1, replica_groups=mesh['row'=32,'col'=16] {'col'}, dimensions={1}, use_global_device_ids=true | all-gather | bytes 278528 | tf_op jit(solution)/shard_map/all_gather | solution.py:82
  26.9 15.4 %collective-permute-start = (bf16[512,256]{0,1:T(8,128)(2,1)S(1)}, bf16[512,256]{0,1:T(8,128)(2,1)S(1)}, u32[]{:S(2)}, u32[]{:S(2)}) collective-permute-start(bf16[512,256]{0,1:T(8,128)(2,1)S(1)} %all_gather.9), channel_id=1, source_target_pairs={{0,256},{16,272},{32,288},{48,304},{64,320},{80,336},{96,352},{112... | collective-permute-start | bytes 786440 | tf_op jit(solution)/shard_map/ppermute | solution.py:31
  51.1 226.5 %all-reduce.12.cloned.1.call-done = (bf16[512,512]{1,0:T(8,128)(2,1)}, bf16[512,512]{1,0:T(8,128)(2,1)}) async-done(((bf16[512,512]{1,0:T(8,128)(2,1)}, bf16[512,512]{1,0:T(8,128)(2,1)}), (bf16[512,512]{1,0:T(8,128)(2,1)}, bf16[512,512]{1,0:T(8,128)(2,1)})) %all-reduce.12.cloned.1.call-update) | async-done | bytes 1048592 | tf_op jit(solution)/shard_map/psum | solution.py:36
  289.9 194.6 %all_gather.10 = f32[4096,16]{1,0:T(8,128)S(1)} all-gather(f32[8,16]{1,0:T(8,128)S(1)} %copy.33), channel_id=1, replica_groups=mesh['row'=32,'col'=16] {'row','col'}, dimensions={0}, use_global_device_ids=true | all-gather | bytes 262656 | tf_op jit(solution)/shard_map/all_gather | solution.py:126
  486.0 11.7 cholesky.130
  497.7 9.8 custom-call.13
  511.3 11.7 cholesky.147
  544.9 6.7 collective-permute-start.12
  553.6 6.7 collective-permute-start.13
  566.4 6.7 collective-permute-start.14
  575.0 19.7 %custom-call.14 = f32[2,128,128]{1,2,0:T(8,128)S(1)} custom-call(f32[2,128,128]{2,1,0:T(8,128)S(1)} %get-tuple-element.91), custom_call_target="InvertDiagBlocksLowerTriangular" | custom-call | tf_op jit(solution)/shard_map/triangular_solve/custom-call.0 | solution.py:61
  594.8 6.7 collective-permute-start.15
  606.6 211.2 %all-reduce.10.cloned.1.call-done = (bf16[512,256]{0,1:T(8,128)(2,1)}, bf16[512,256]{0,1:T(8,128)(2,1)}) async-done(((bf16[512,256]{0,1:T(8,128)(2,1)}, bf16[512,256]{0,1:T(8,128)(2,1)}), (bf16[512,256]{0,1:T(8,128)(2,1)}, bf16[512,256]{0,1:T(8,128)(2,1)})) %all-reduce.10.cloned.1.call-update) | async-done | bytes 524304 | tf_op jit(solution)/shard_map/psum | solution.py:36
  839.6 194.8 %all_gather.11 = f32[4096,16]{1,0:T(8,128)S(1)} all-gather(f32[8,16]{1,0:T(8,128)S(1)} %copy.38), channel_id=1, replica_groups=mesh['row'=32,'col'=16] {'row','col'}, dimensions={0}, use_global_device_ids=true | all-gather | bytes 262656 | tf_op jit(solution)/shard_map/all_gather | solution.py:126
  1038.7 11.7 cholesky.164
  1050.5 9.8 custom-call.15
  1063.9 11.7 cholesky.181
  1077.6 6.7 collective-permute-start.25
  1097.4 6.7 collective-permute-start.27
  1106.1 6.7 collective-permute-start.28
  1118.8 6.7 collective-permute-start.29
  1127.4 19.7 %custom-call.16 = f32[2,128,128]{1,2,0:T(8,128)S(1)} custom-call(f32[2,128,128]{2,1,0:T(8,128)S(1)} %get-tuple-element.92), custom_call_target="InvertDiagBlocksLowerTriangular" | custom-call | tf_op jit(solution)/shard_map/triangular_solve/custom-call.0 | solution.py:61
  1147.2 6.7 collective-permute-start.30
  1158.5 212.0 %all-reduce.8.cloned.1.call-done = (bf16[512,256]{0,1:T(8,128)(2,1)}, bf16[512,256]{0,1:T(8,128)(2,1)}) async-done(((bf16[512,256]{0,1:T(8,128)(2,1)}, bf16[512,256]{0,1:T(8,128)(2,1)}), (bf16[512,256]{0,1:T(8,128)(2,1)}, bf16[512,256]{0,1:T(8,128)(2,1)})) %all-reduce.8.cloned.1.call-update) | async-done | bytes 524304 | tf_op jit(solution)/shard_map/psum | solution.py:36
  (212 shorter events, 147.0 us)
Async XLA Ops:
  7.2 270.4 %all-reduce.12.cloned.1.call-start = ((), (), s32[]{:S(2)}) async-start(), calls=%async_computation.2 | async-start | bytes 2097152 | tf_op jit(solution)/shard_map/psum | solution.py:36
  26.9 20.5 %collective-permute-start = (bf16[512,256]{0,1:T(8,128)(2,1)S(1)}, bf16[512,256]{0,1:T(8,128)(2,1)S(1)}, u32[]{:S(2)}, u32[]{:S(2)}) collective-permute-start(bf16[512,256]{0,1:T(8,128)(2,1)S(1)} %all_gather.9), channel_id=1, source_target_pairs={{0,256},{16,272},{32,288},{48,304},{64,320},{80,336},{96,352},{112... | collective-permute-start | bytes 786440 | tf_op jit(solution)/shard_map/ppermute | solution.py:31
  49.5 768.3 %all-reduce.10.cloned.1.call-start = ((), (), s32[]{:S(2)}) async-start(), calls=%async_computation.1 | async-start | bytes 1048576 | tf_op jit(solution)/shard_map/psum | solution.py:36
  281.2 226.6 %collective-permute-start.1 = (f32[512,16]{0,1:T(8,128)S(1)}, f32[512,16]{0,1:T(8,128)S(1)}, u32[]{:S(2)}, u32[]{:S(2)}) collective-permute-start(f32[512,16]{0,1:T(8,128)S(1)} %pad_maximum_fusion.1), channel_id=1, source_target_pairs={{0,1},{1,2},{2,3},{3,4},{4,5},{5,6},{6,7},{7,8},{8,9},{9,10},{10,1... | collective-permute-start | bytes 98312 | tf_op jit(solution)/shard_map/ppermute | solution.py:18
  284.3 240.6 %collective-permute-start.9 = (f32[512,16]{0,1:T(8,128)S(1)}, f32[512,16]{0,1:T(8,128)S(1)}, u32[]{:S(2)}, u32[]{:S(2)}) collective-permute-start(f32[512,16]{0,1:T(8,128)S(1)} %pad_maximum_fusion.1), channel_id=1, source_target_pairs={{0,15},{1,0},{2,1},{3,2},{4,3},{5,4},{6,5},{7,6},{8,7},{9,8},{10,9... | collective-permute-start | bytes 98312 | tf_op jit(solution)/shard_map/ppermute | solution.py:20
  507.8 15.2 %collective-permute-start.2 = (f32[512,16]{0,1:T(8,128)S(1)}, f32[512,16]{0,1:T(8,128)S(1)}, u32[]{:S(2)}, u32[]{:S(2)}) collective-permute-start(f32[512,16]{0,1:T(8,128)S(1)} %collective-permute-done.1), channel_id=1, source_target_pairs={{0,1},{1,2},{2,3},{3,4},{4,5},{5,6},{6,7},{7,8},{8,9},{9,10},{10,1... | collective-permute-start | bytes 98312 | tf_op jit(solution)/shard_map/ppermute | solution.py:18
  525.0 9.3 collective-permute-start.10
  531.7 9.3 collective-permute-start.4
  534.3 10.6 collective-permute-start.11
  541.0 10.6 collective-permute-start.5
  553.6 12.8 collective-permute-start.13
  560.3 12.8 collective-permute-start.7
  566.4 28.5 %collective-permute-start.14 = (f32[512,16]{0,1:T(8,128)S(1)}, f32[512,16]{0,1:T(8,128)S(1)}, u32[]{:S(2)}, u32[]{:S(2)}) collective-permute-start(f32[512,16]{0,1:T(8,128)S(1)} %collective-permute-done.13), channel_id=1, source_target_pairs={{0,15},{1,0},{2,1},{3,2},{4,3},{5,4},{6,5},{7,6},{8,7},{9,8},{10,9... | collective-permute-start | bytes 98312 | tf_op jit(solution)/shard_map/ppermute | solution.py:20
  573.1 28.5 %collective-permute-start.8 = (f32[512,16]{0,1:T(8,128)S(1)}, f32[512,16]{0,1:T(8,128)S(1)}, u32[]{:S(2)}, u32[]{:S(2)}) collective-permute-start(f32[512,16]{0,1:T(8,128)S(1)} %collective-permute-done.7), channel_id=1, source_target_pairs={{0,1},{1,2},{2,3},{3,4},{4,5},{5,6},{6,7},{7,8},{8,9},{9,10},{10,1... | collective-permute-start | bytes 98312 | tf_op jit(solution)/shard_map/ppermute | solution.py:18
  605.1 765.4 %all-reduce.8.cloned.1.call-start = ((), (), s32[]{:S(2)}) async-start(), calls=%async_computation | async-start | bytes 1048576 | tf_op jit(solution)/shard_map/psum | solution.py:36
  830.9 229.6 %collective-permute-start.16 = (f32[512,16]{0,1:T(8,128)S(1)}, f32[512,16]{0,1:T(8,128)S(1)}, u32[]{:S(2)}, u32[]{:S(2)}) collective-permute-start(f32[512,16]{0,1:T(8,128)S(1)} %pad_maximum_fusion.2), channel_id=1, source_target_pairs={{0,1},{1,2},{2,3},{3,4},{4,5},{5,6},{6,7},{7,8},{8,9},{9,10},{10,1... | collective-permute-start | bytes 98312 | tf_op jit(solution)/shard_map/ppermute | solution.py:18
  834.0 243.6 %collective-permute-start.24 = (f32[512,16]{0,1:T(8,128)S(1)}, f32[512,16]{0,1:T(8,128)S(1)}, u32[]{:S(2)}, u32[]{:S(2)}) collective-permute-start(f32[512,16]{0,1:T(8,128)S(1)} %pad_maximum_fusion.2), channel_id=1, source_target_pairs={{0,15},{1,0},{2,1},{3,2},{4,3},{5,4},{6,5},{7,6},{8,7},{9,8},{10,9... | collective-permute-start | bytes 98312 | tf_op jit(solution)/shard_map/ppermute | solution.py:20
  1060.5 15.1 %collective-permute-start.17 = (f32[512,16]{0,1:T(8,128)S(1)}, f32[512,16]{0,1:T(8,128)S(1)}, u32[]{:S(2)}, u32[]{:S(2)}) collective-permute-start(f32[512,16]{0,1:T(8,128)S(1)} %collective-permute-done.16), channel_id=1, source_target_pairs={{0,1},{1,2},{2,3},{3,4},{4,5},{5,6},{6,7},{7,8},{8,9},{9,10},{10,1... | collective-permute-start | bytes 98312 | tf_op jit(solution)/shard_map/ppermute | solution.py:18
  1086.9 10.6 collective-permute-start.26
  1093.6 10.6 collective-permute-start.20
  1106.1 12.7 collective-permute-start.28
  1112.8 12.7 collective-permute-start.22
  1118.8 28.5 %collective-permute-start.29 = (f32[512,16]{0,1:T(8,128)S(1)}, f32[512,16]{0,1:T(8,128)S(1)}, u32[]{:S(2)}, u32[]{:S(2)}) collective-permute-start(f32[512,16]{0,1:T(8,128)S(1)} %collective-permute-done.28), channel_id=1, source_target_pairs={{0,15},{1,0},{2,1},{3,2},{4,3},{5,4},{6,5},{7,6},{8,7},{9,8},{10,9... | collective-permute-start | bytes 98312 | tf_op jit(solution)/shard_map/ppermute | solution.py:20
  1125.5 28.5 %collective-permute-start.23 = (f32[512,16]{0,1:T(8,128)S(1)}, f32[512,16]{0,1:T(8,128)S(1)}, u32[]{:S(2)}, u32[]{:S(2)}) collective-permute-start(f32[512,16]{0,1:T(8,128)S(1)} %collective-permute-done.22), channel_id=1, source_target_pairs={{0,1},{1,2},{2,3},{3,4},{4,5},{5,6},{6,7},{7,8},{8,9},{9,10},{10,1... | collective-permute-start | bytes 98312 | tf_op jit(solution)/shard_map/ppermute | solution.py:18
  (17 other events, 367.5 us)
Sparse Core Ops, SparseCore 0:
  49.6 227.9 all-reduce.11
  605.2 212.4 all-reduce.9
  1157.9 212.5 all-reduce.7
